TPU v7x, 32 devices: a whole 2x2x4 slice. The times are simulated.
32 devices in a mesh: ctx: 8 (over z, x), head: 4 (over y, core).
Axes of the slice: x: 2, y: 2, z: 4, core: 2. Of those that a mesh axis runs over, the one named last changes fastest.
Arguments:
- probe_vectors: bfloat16 [1024, 8192], P('ctx', 'head'), may hold values from -160 to 160
- lookup_tensor: bfloat16 [8192, 1024], P('ctx', 'head'), may hold values from -4.5 to 4.5
- payload_tensor: bfloat16 [8192, 1024], P('ctx', 'head'), may hold values from -6 to 6
- sequence_locations: int32 [1024], replicated, may hold values from 0 to 8191, as said below
- attention_return_matrix: bfloat16 [8192, 8192], P('head', 'ctx'), may hold values from -0.0625 to 0.0625
- skip_stream_state: bfloat16 [1024, 8192], P('head', 'ctx'), may hold values from -4 to 4
- early_rescaling_factor: float32 [8192], P('ctx'), may hold values from 0.5 to 1.5
- lexicon_projection_matrix: bfloat16 [8192, 65536], P(None, ('ctx', 'head')), may hold values from -0.1875 to 0.1875
- calibrating_divisor: float32 [1024], replicated, may hold values from 0.02 to 1
- desired_tokens_list: int32 [1024], replicated, may hold values from 0 to 65535
Outputs:
- hidden: bfloat16 [1024, 8192], P('head', 'ctx')
- logprob: float32 [1024], replicated
Inputs may be any that keep to these rules, and one draw needn't show every extreme that they name: `sequence_locations`: query i stands at a position from i * 8 to (i + 1) * 8 - 1; the last query stands at 8191.
All inputs are finite; a program needn't handle non-finite values.
Results may differ from a plain program's by a relative error of at most 0.0014.
The roundings to bfloat16 on the way count: a program that leaves them out, or rounds other values in their place, can miss the bound.
Values may be sent and summed in bfloat16 or wider, within the bound.
No kernel may reach another device: no remote copies, remote signals or barrier semaphores. Data moves between devices by JAX's collectives and lax.ppermute only.
A program may use at most 192 MiB of HBM per device.

v0:
```python
import jax
import jax.numpy as jnp
from jax import lax
from jax.sharding import PartitionSpec as P

D = 8192
QUERY_HEAD_COUNT = 64
KEY_VALUE_HEADS = 8
HEAD_SIZE = 128


neg_big = -1e30
eps = 1e-05


def local_attention(every_query, lookup_tensor, payload_tensor, sequence_locations, key_start):
    total_rows = every_query.shape[0]
    ctx_len = lookup_tensor.shape[0]
    kv_here = lookup_tensor.shape[1] // HEAD_SIZE
    group_size = QUERY_HEAD_COUNT // KEY_VALUE_HEADS
    scale_factor = HEAD_SIZE ** (-0.5)
    row_block = min(512, total_rows)
    query_heads = every_query.reshape(total_rows, kv_here, group_size, HEAD_SIZE)
    key_heads = lookup_tensor.reshape(ctx_len, kv_here, HEAD_SIZE)
    value_heads = payload_tensor.reshape(ctx_len, kv_here, HEAD_SIZE)
    key_pos = key_start + jnp.arange(ctx_len, dtype=jnp.int32)
    maxima, sums, accums = ([], [], [])
    for row_start in range(0, total_rows, row_block):
        row_pos = sequence_locations[row_start : row_start + row_block]
        visible = key_pos[None, None, :] <= row_pos[:, None, None]
        head_max, head_sum, head_acc = ([], [], [])
        for kv_head in range(kv_here):
            scores = (
                jnp.einsum(
                    "qhd,kd->qhk",
                    query_heads[row_start : row_start + row_block, kv_head],
                    key_heads[:, kv_head],
                    preferred_element_type=jnp.float32,
                )
                * scale_factor
            )
            block_max = jnp.max(jnp.where(visible, scores, neg_big), axis=-1)
            weights = jnp.where(visible, jnp.exp(scores - block_max[..., None]), 0.0)
            head_sum.append(jnp.sum(weights, axis=-1))
            head_max.append(block_max)
            head_acc.append(
                jnp.einsum(
                    "qhk,kd->qhd",
                    weights.astype(jnp.bfloat16),
                    value_heads[:, kv_head],
                    preferred_element_type=jnp.float32,
                )
            )
        maxima.append(jnp.concatenate(head_max, axis=1))
        sums.append(jnp.concatenate(head_sum, axis=1))
        accums.append(jnp.concatenate(head_acc, axis=1))
    return (
        jnp.concatenate(maxima, axis=0),
        jnp.concatenate(sums, axis=0),
        jnp.concatenate(accums, axis=0),
    )


def shards(
    probe_vectors,
    lookup_tensor,
    payload_tensor,
    sequence_locations,
    attention_return_matrix,
    skip_stream_state,
    early_rescaling_factor,
    lexicon_projection_matrix,
    calibrating_divisor,
    desired_tokens_list,
):
    heads_here = probe_vectors.shape[1] // HEAD_SIZE
    every_query = lax.all_gather(probe_vectors, "ctx", axis=0, tiled=True)
    key_start = lax.axis_index("ctx") * lookup_tensor.shape[0]
    local_max, local_sum, local_acc = local_attention(
        every_query, lookup_tensor, payload_tensor, sequence_locations, key_start
    )
    global_max = lax.pmax(local_max.astype(jnp.bfloat16), "ctx").astype(local_max.dtype)
    rescale = jnp.exp(local_max - global_max)
    acc_rows, sum_rows = (
        lax.psum_scatter(local_acc * rescale[..., None], "ctx", scatter_dimension=0, tiled=True),
        lax.psum_scatter(local_sum * rescale, "ctx", scatter_dimension=0, tiled=True),
    )
    attn = (
        (acc_rows / sum_rows[..., None])
        .astype(jnp.bfloat16)
        .reshape(acc_rows.shape[0], heads_here * HEAD_SIZE)
    )
    mixed_part = jnp.dot(
        lax.all_gather(attn, "ctx", axis=0, tiled=True),
        attention_return_matrix,
        preferred_element_type=jnp.float32,
    )
    mixed_rows = lax.psum_scatter(mixed_part, "head", scatter_dimension=0, tiled=True)
    hidden = (skip_stream_state.astype(jnp.float32) + mixed_rows).astype(jnp.bfloat16)
    widened = hidden.astype(jnp.float32)
    square_total = lax.psum(jnp.sum(widened * widened, axis=1), "ctx")
    normed = (
        widened * lax.rsqrt(square_total / D + eps)[:, None] * early_rescaling_factor[None, :]
    ).astype(jnp.bfloat16)
    full_rows = lax.all_gather(normed, "ctx", axis=1, tiled=True)
    early_class_energies = jnp.dot(
        lax.all_gather(full_rows, "head", axis=0, tiled=True),
        lexicon_projection_matrix,
        preferred_element_type=jnp.float32,
    )
    tempered_affinities = early_class_energies / calibrating_divisor[:, None]
    vocab_here = lexicon_projection_matrix.shape[1]
    offset = (lax.axis_index("ctx") * lax.axis_size("head") + lax.axis_index("head")) * vocab_here
    column_ids = jnp.arange(vocab_here, dtype=jnp.int32)[None, :] + offset
    picked = jnp.sum(
        jnp.where(column_ids == desired_tokens_list[:, None], tempered_affinities, 0.0), axis=1
    )
    local_peak = jnp.max(tempered_affinities, axis=1)
    peak = lax.pmax(local_peak, ("ctx", "head"))
    total, target_logit = lax.psum(
        (jnp.sum(jnp.exp(tempered_affinities - peak[:, None]), axis=1), picked), ("ctx", "head")
    )
    logprob = target_logit - peak - jnp.log(total)
    return (hidden, logprob)


def solution(mesh):
    placed = (
        P("ctx", "head"),
        P("ctx", "head"),
        P("ctx", "head"),
        P(),
        P("head", "ctx"),
        P("head", "ctx"),
        P("ctx"),
        P(None, ("ctx", "head")),
        P(),
        P(),
    )
    return jax.shard_map(
        shards, mesh=mesh, in_specs=placed, out_specs=(P("head", "ctx"), P()), check_vma=False
    )
```

profile of v0, /device:TPU:0, one launch (start us, length us, event | category | flops | bytes accessed | tf_op | source)
XLA Modules:
  0.0 878.8 jit_solution(8990251536320615546)
XLA Ops:
  7.2 0.0 all-gather.5.cloned.1.call-start
  7.2 2.0 copy.12
  9.3 0.0 all-gather.5.cloned.1.call-update
  9.3 0.0 reduce-scatter.6.cloned.1.call-start
  9.3 1.2 copy.14
  10.6 2.2 copy.16
  12.8 0.8 fusion.36
  13.6 0.7 broadcast_compare_fusion.1
  14.3 73.7 %all-gather.5.cloned.1.call-done = bf16[1024,2048]{0,1:T(8,128)(2,1)} async-done(((bf16[128,2048]{0,1:T(8,128)(2,1)}), bf16[1024,2048]{0,1:T(8,128)(2,1)}) %all-gather.5.cloned.1.call-update) | async-done | bytes 4194320 | tf_op jit(solution)/shard_map/all_gather | solution.py:77
  88.0 8.8 select_reduce_fusion.1
  96.8 15.3 %fusion.4 = (f32[512,8]{0,1:T(8,128)S(1)}, f32[512,8]{0,1:T(8,128)S(1)}, f32[512,8,1024]{2,0,1:T(8,128)}) fusion(f32[512,8,1024]{2,0,1:T(8,128)} %get-tuple-element.19, f32[512,8]{0,1:T(8,128)S(1)} %get-tuple-element.18, pred[512,1024]{1,0:T(8,128)(4,1)S(1)} %get-tuple-element.15, bf16[1024,2,128]{0,2,1:T(8,128)(2,1)S(1)} %bitcast.76, ...), kind=kOutput, calls=%fused_computation.12 | convolution fusion | flops 1103093760 | bytes 35438592 | tf_op jit(solution)/shard_map/qhd,kd->qhk/dot_general | solution.py:34
  112.1 7.6 fusion.10
  119.7 7.4 select_reduce_fusion.3
  127.1 14.7 %fusion = (f32[512,8]{0,1:T(8,128)S(1)}, f32[512,8]{0,1:T(8,128)S(1)}, f32[512,8,1024]{2,0,1:T(8,128)}) fusion(f32[512,8,1024]{2,0,1:T(8,128)} %get-tuple-element.22, f32[512,8]{0,1:T(8,128)S(1)} %get-tuple-element.21, pred[512,1024]{1,0:T(8,128)(4,1)S(1)} %get-tuple-element.14, bf16[1024,2,128]{0,2,1:T(8,128)(2,1)} %bitcast.77, ...), kind=kOutput, calls=%fused_computation.8 | convolution fusion | flops 1103093760 | bytes 35438592 | tf_op jit(solution)/shard_map/qhd,kd->qhk/dot_general | solution.py:34
  141.8 8.9 %fusion.14 = f32[512,8,128]{2,0,1:T(8,128)} fusion(f32[512,8,1024]{2,0,1:T(8,128)} %get-tuple-element.22, f32[512,8]{0,1:T(8,128)S(1)} %get-tuple-element.21, pred[512,1024]{1,0:T(8,128)(4,1)S(1)} %get-tuple-element.14, bf16[1024,2,128]{0,2,1:T(8,128)(2,1)} %bitcast.71), kind=kOutput, calls=%fused_computation.22 | convolution fusion | flops 1090519040 | bytes 19677184 | tf_op jit(solution)/shard_map/qhk,kd->qhd/dot_general | solution.py:47
  150.7 4.6 fusion.8
  155.3 8.5 fusion.12
  163.8 11.1 %fusion.2 = (f32[512,8]{0,1:T(8,128)S(1)}, f32[512,8]{0,1:T(8,128)S(1)}) fusion(f32[512,8,1024]{2,0,1:T(8,128)} %get-tuple-element.23, f32[512,8]{0,1:T(8,128)S(1)} %get-tuple-element.5, pred[512,1024]{1,0:T(8,128)(4,1)S(1)} %get-tuple-element.14, f32[512,8]{0,1:T(8,128)S(1)} %get-tuple-element.7, f32[512,8,1024]{2,0,1:T(8,128)S(1)} %bitcast.69, ...), kind=kLoop, calls=%fused_computation.10 | loop fusion | flops 33546240 | bytes 34668544 | tf_op jit(solution)/shard_map/reduce_sum | solution.py:44
  174.9 34.3 %pmax.14 = bf16[1024,16]{0,1:T(8,128)(2,1)S(1)} all-reduce(bf16[1024,16]{0,1:T(8,128)(2,1)S(1)} %fusion.27), channel_id=1, replica_groups=mesh['ctx'=8,'head'=4] {'ctx'}, use_global_device_ids=true, to_apply=%region_4.5 | all-reduce | flops 16384 | bytes 65536 | tf_op jit(solution)/shard_map/pmax | solution.py:82
  209.2 0.7 maximum_multiply_fusion.1
  209.8 0.0 reduce-scatter.6.cloned.1.call-update
  209.9 0.0 reduce-scatter.4.cloned.1.call-start
  209.9 8.0 maximum_multiply_fusion
  217.9 0.0 reduce-scatter.4.cloned.1.call-update
  218.0 0.0 all-gather.7.cloned.1.call-start
  218.0 44.1 %reduce-scatter.6.cloned.1.call-done = f32[128,16]{0,1:T(8,128)} async-done(((f32[1024,16]{0,1:T(8,128)}), f32[128,16]{0,1:T(8,128)}) %reduce-scatter.6.cloned.1.call-update) | async-done | bytes 8208 | tf_op jit(solution)/shard_map/reduce_scatter | solution.py:86
  262.1 150.6 %reduce-scatter.4.cloned.1.call-done = f32[128,16,128]{2,0,1:T(8,128)} async-done(((f32[1024,16,128]{2,0,1:T(8,128)}), f32[128,16,128]{2,0,1:T(8,128)}) %reduce-scatter.4.cloned.1.call-update) | async-done | bytes 1048592 | tf_op jit(solution)/shard_map/reduce_scatter | solution.py:85
  412.6 1.6 divide_convert_fusion
  414.2 1.0 copy.23
  415.2 0.0 all-gather.7.cloned.1.call-update
  415.3 0.3 reduce-scatter.8.cloned.1.call-start
  415.5 73.6 %all-gather.7.cloned.1.call-done = bf16[1024,2048]{0,1:T(8,128)(2,1)} async-done(((bf16[128,2048]{0,1:T(8,128)(2,1)}), bf16[1024,2048]{0,1:T(8,128)(2,1)}) %all-gather.7.cloned.1.call-update) | async-done | bytes 4194320 | tf_op jit(solution)/shard_map/all_gather | solution.py:94
  489.1 10.0 %fusion.38 = f32[1024,1024]{1,0:T(8,128)} fusion(bf16[1024,2048]{0,1:T(8,128)(2,1)} %all-gather.7.cloned.1.call-done, bf16[2048,1024]{1,0:T(8,128)(2,1)} %param.14), kind=kOutput, calls=%fused_computation.67 | convolution fusion | flops 4294967296 | bytes 12582912 | tf_op jit(solution)/shard_map/dot_general | solution.py:93
  499.1 0.0 reduce-scatter.8.cloned.1.call-update
  499.1 0.0 all-gather.9.cloned.1.call-start
  499.2 42.9 %reduce-scatter.8.cloned.1.call-done = f32[256,1024]{1,0:T(8,128)} async-done(((f32[1024,1024]{1,0:T(8,128)}), f32[256,1024]{1,0:T(8,128)}) %reduce-scatter.8.cloned.1.call-update) | async-done | bytes 1048592 | tf_op jit(solution)/shard_map/reduce_scatter | solution.py:98
  542.0 1.5 fusion.20
  543.5 21.4 %psum.21 = f32[256]{0:T(256)S(1)} all-reduce(f32[256]{0:T(256)S(1)} %get-tuple-element.10), channel_id=1, replica_groups=mesh['ctx'=8,'head'=4] {'ctx'}, use_global_device_ids=true, to_apply=%region_13.14 | all-reduce | flops 256 | bytes 2048 | tf_op jit(solution)/shard_map/psum | solution.py:101
  564.9 1.0 fusion.22
  565.9 0.0 all-gather.9.cloned.1.call-update
  565.9 0.0 all-gather.11.cloned.1.call-start
  566.0 69.2 %all-gather.9.cloned.1.call-done = bf16[256,8192]{1,0:T(8,128)(2,1)} async-done(((bf16[256,1024]{1,0:T(8,128)(2,1)}), bf16[256,8192]{1,0:T(8,128)(2,1)}) %all-gather.9.cloned.1.call-update) | async-done | bytes 4194320 | tf_op jit(solution)/shard_map/all_gather | solution.py:105
  635.2 106.0 %all-gather.11.cloned.1.call-done = bf16[1024,8192]{1,0:T(8,128)(2,1)} async-done(((bf16[256,8192]{1,0:T(8,128)(2,1)}), bf16[1024,8192]{1,0:T(8,128)(2,1)}) %all-gather.11.cloned.1.call-update) | async-done | bytes 16777232 | tf_op jit(solution)/shard_map/all_gather | solution.py:107
  741.2 45.0 %fusion.37 = (f32[1024]{0:T(1024)S(1)}, f32[1024,2048]{1,0:T(8,128)}) fusion(f32[1024]{0:T(1024)S(1)} %copy-done.9, bf16[1024,8192]{1,0:T(8,128)(2,1)} %all-gather.11.cloned.1.call-done, bf16[8192,2048]{1,0:T(8,128)(2,1)} %param.17), kind=kOutput, calls=%fused_computation.66 | convolution fusion | flops 34363932672 | bytes 58728448 | tf_op jit(solution)/shard_map/dot_general | solution.py:106
  786.2 39.5 %pmax.15 = f32[1024]{0:T(1024)S(1)} all-reduce(f32[1024]{0:T(1024)S(1)} %get-tuple-element.24), channel_id=1, replica_groups=mesh['ctx'=8,'head'=4] {'ctx','head'}, use_global_device_ids=true, to_apply=%region_17.18 | all-reduce | flops 1024 | bytes 8192 | tf_op jit(solution)/shard_map/pmax | solution.py:119
  825.6 4.7 select_reduce_fusion.4
  830.4 41.0 %all-reduce = (f32[1024]{0:T(1024)S(1)}, f32[1024]{0:T(1024)S(1)}) all-reduce(f32[1024]{0:T(1024)S(1)} %get-tuple-element.3, f32[1024]{0:T(1024)S(1)} %get-tuple-element.2), channel_id=1, replica_groups=mesh['ctx'=8,'head'=4] {'ctx','head'}, use_global_device_ids=true, to_apply=%region_19.20 | all-reduce | flops 2048 | bytes 16384 | tf_op jit(solution)/shard_map/psum | solution.py:120
  871.4 0.6 log_subtract_fusion
  (34 shorter events, 0.1 us)
Async XLA Ops:
  7.2 80.8 %all-gather.5.cloned.1.call-start = ((), (), s32[]{:S(2)}) async-start(), calls=%async_computation.3 | async-start | bytes 4718592 | tf_op jit(solution)/shard_map/all_gather | solution.py:77
  9.3 252.8 %reduce-scatter.6.cloned.1.call-start = ((), (), s32[]{:S(2)}) async-start(), calls=%async_computation.5 | async-start | bytes 73728 | tf_op jit(solution)/shard_map/reduce_scatter | solution.py:86
  10.6 101.5 %copy-start.3 = (bf16[1024,256]{0,1:T(8,128)(2,1)}, bf16[1024,256]{0,1:T(8,128)(2,1)S(1)}, u32[]{:S(2)}) copy-start(bf16[1024,256]{0,1:T(8,128)(2,1)S(1)} %copy.14) | copy-start | bytes 1572868
  88.0 8.8 copy-start.8
  96.8 15.3 %copy-start.1 = (bf16[1024,256]{0,1:T(8,128)(2,1)S(1)}, bf16[1024,256]{0,1:T(8,128)(2,1)}, u32[]{:S(2)}) copy-start(bf16[1024,256]{0,1:T(8,128)(2,1)} %copy.16) | copy-start | bytes 1572868
  112.1 7.6 copy-start.4
  127.1 23.5 %slice-start = ((s8[16777216]{0:T(1024)(128)(4,1)}), s8[4194304]{0:T(1024)(128)(4,1)S(1)}, s32[]{:S(2)}) async-start(s8[16777216]{0:T(1024)(128)(4,1)} %bitcast.68), calls=%async_computation.10 | async-start | bytes 8388608
  127.1 23.5 %slice-start.1 = ((s8[16777216]{0:T(1024)(128)(4,1)}), s8[4194304]{0:T(1024)(128)(4,1)S(1)}, s32[]{:S(2)}) async-start(s8[16777216]{0:T(1024)(128)(4,1)} %bitcast.68), calls=%async_computation.11 | async-start | bytes 8388608
  127.1 23.5 %slice-start.2 = ((s8[16777216]{0:T(1024)(128)(4,1)}), s8[4194304]{0:T(1024)(128)(4,1)S(1)}, s32[]{:S(2)}) async-start(s8[16777216]{0:T(1024)(128)(4,1)} %bitcast.68), calls=%async_computation.12 | async-start | bytes 8388608
  141.8 8.9 %slice-start.3 = ((s8[16777216]{0:T(1024)(128)(4,1)}), s8[4194304]{0:T(1024)(128)(4,1)S(1)}, s32[]{:S(2)}) async-start(s8[16777216]{0:T(1024)(128)(4,1)} %bitcast.68), calls=%async_computation.13 | async-start | bytes 8388608
  141.8 8.9 %copy-start.2 = (bf16[1024,256]{0,1:T(8,128)(2,1)S(1)}, bf16[1024,256]{0,1:T(8,128)(2,1)}, u32[]{:S(2)}) copy-start(bf16[1024,256]{0,1:T(8,128)(2,1)} %copy.16) | copy-start | bytes 1572868
  209.9 202.8 %reduce-scatter.4.cloned.1.call-start = ((), (), s32[]{:S(2)}) async-start(), calls=%async_computation.4 | async-start | bytes 9437184 | tf_op jit(solution)/shard_map/reduce_scatter | solution.py:85
  217.9 324.1 %copy-start.5 = (bf16[256,1024]{1,0:T(8,128)(2,1)S(1)}, bf16[256,1024]{1,0:T(8,128)(2,1)}, u32[]{:S(2)}) copy-start(bf16[256,1024]{1,0:T(8,128)(2,1)} %param.15) | copy-start | bytes 1572868
  218.0 346.9 %copy-start.7 = (f32[1024]{0:T(1024)S(1)}, f32[1024]{0:T(1024)}, u32[]{:S(2)}) copy-start(f32[1024]{0:T(1024)} %param.16) | copy-start | bytes 12292
  218.0 271.2 %all-gather.7.cloned.1.call-start = ((), (), s32[]{:S(2)}) async-start(), calls=%async_computation.6 | async-start | bytes 4718592 | tf_op jit(solution)/shard_map/all_gather | solution.py:94
  415.2 325.9 %copy-start.9 = (f32[1024]{0:T(1024)S(1)}, f32[1024]{0:T(1024)}, u32[]{:S(2)}) copy-start(f32[1024]{0:T(1024)} %param.18) | copy-start | bytes 12292
  415.3 126.8 %reduce-scatter.8.cloned.1.call-start = ((), (), s32[]{:S(2)}) async-start(), calls=%async_computation.7 | async-start | bytes 5242880 | tf_op jit(solution)/shard_map/reduce_scatter | solution.py:98
  499.1 136.0 %all-gather.9.cloned.1.call-start = ((), (), s32[]{:S(2)}) async-start(), calls=%async_computation.8 | async-start | bytes 4718592 | tf_op jit(solution)/shard_map/all_gather | solution.py:105
  543.5 242.7 %copy-start = (bf16[256,1024]{1,0:T(8,128)(2,1)}, bf16[256,1024]{1,0:T(8,128)(2,1)S(1)}, u32[]{:S(2)}) copy-start(bf16[256,1024]{1,0:T(8,128)(2,1)S(1)} %get-tuple-element.11) | copy-start | bytes 1572868
  565.9 175.3 %all-gather.11.cloned.1.call-start = ((), (), s32[]{:S(2)}) async-start(), calls=%async_computation.9 | async-start | bytes 20971520 | tf_op jit(solution)/shard_map/all_gather | solution.py:107
  635.2 190.4 %copy-start.6 = (s32[1024]{0:T(1024)S(1)}, s32[1024]{0:T(1024)}, u32[]{:S(2)}) copy-start(s32[1024]{0:T(1024)} %param.19) | copy-start | bytes 12292
Sparse Core Ops, SparseCore 0:
  10.6 77.3 all-gather.4
  210.0 52.0 reduce-scatter.5
  265.7 146.8 reduce-scatter.3
  415.4 73.7 all-gather.6
  499.2 42.7 reduce-scatter.7
  566.0 69.0 all-gather.8
  636.7 104.4 all-gather.10
where the time goes:
time: 879 us
  waiting for transfers between devices  560 us (64%)
  blocking collectives  136 us (15%)
  matrix products  131 us (15%)
  other arithmetic  29.8 us (3%)
  between operations  14.3 us (2%)
    reduce_scatter x1, waiting for transfers between devices, shards(): lax.psum_scatter(local_acc * rescale[..., None], 'ctx', scatter_dimension...  151 us
    all_gather x1, waiting for transfers between devices, shards(): lax.all_gather(full_rows, 'head', axis=0, tiled=True)  106 us
    all_gather x1, waiting for transfers between devices, shards(): every_query = lax.all_gather(probe_vectors, 'ctx', axis=0, tiled=True)  73.7 us
    all_gather x1, waiting for transfers between devices, shards(): lax.all_gather(attn, 'ctx', axis=0, tiled=True)  73.6 us
    all_gather x1, waiting for transfers between devices, shards(): full_rows = lax.all_gather(normed, 'ctx', axis=1, tiled=True)  69.2 us
    dot_general x4, matrix products, local_attention(): jnp.einsum('qhd,kd->qhk', query_heads[row_start:row_start + row_block, kv...  46.2 us
    dot_general x1, matrix products, shards(): jnp.dot(lax.all_gather(full_rows, 'head', axis=0, tiled=True), lexicon_pr...  45 us
    reduce_scatter x1, waiting for transfers between devices, shards(): lax.psum_scatter(local_sum * rescale, 'ctx', scatter_dimension=0, tiled=T...  44.1 us
  transfers between devices with their start and end apart: 7, of which 7 were waited for; matrix products, arithmetic and copies ran while one was open for 1% of the time, Pallas kernels for 0%

commit v1 on v0

v1 whole, which is shorter than its diff:
```python
import functools
import math

import jax
import jax.numpy as jnp
import numpy as np
from jax import lax
from jax.experimental import pallas as pl
from jax.experimental.pallas import tpu as pltpu
from jax.sharding import PartitionSpec as P

QUERY_HEAD_COUNT = 64
KEY_VALUE_HEADS = 8
HEAD_SIZE = 128

neg_big = -1e30
eps = 1e-05
AXES = ("ctx", "head")


class Moves:
    def __init__(self, mesh):
        self.ctx, self.head = mesh.shape["ctx"], mesh.shape["head"]

    def perm(self, ctx_to=None, head_to=None):
        pairs = []
        for i in range(self.ctx):
            for h in range(self.head):
                i2 = i if ctx_to is None else ctx_to(i)
                h2 = h if head_to is None else head_to(h)
                if i2 is not None and h2 is not None:
                    pairs.append((i * self.head + h, i2 * self.head + h2))
        return pairs

    def ctx_move(self, value, ctx_to):
        return lax.ppermute(value, AXES, self.perm(ctx_to=ctx_to))

    def head_move(self, value, head_to):
        return lax.ppermute(value, AXES, self.perm(head_to=head_to))

    def minor_swap(self, value):
        return self.ctx_move(value, lambda i: i ^ 1)

    def y_swap(self, value):
        return self.head_move(value, lambda h: h ^ 2)

    def core_swap(self, value):
        return self.head_move(value, lambda h: h ^ 1)


def ring_order(count):
    return list(range(0, count, 2)) + list(range(count - 1, 0, -2))


def ring_gather(moves, block, count, ahead, behind):
    order = ring_order(count)
    place = {v: p for p, v in enumerate(order)}

    def shifted(i, step):
        base = i // count * count
        return base + order[(place[i - base] + step) % count]

    def source(step):
        return np.array([shifted(i, step) for i in range(moves.ctx)], np.int32)

    found = [(source(0), block)]
    forward = backward = block
    for k in range(1, max(ahead, behind) + 1):
        if k <= ahead:
            forward = moves.ctx_move(forward, lambda i: shifted(i, 1))
            found.append((source(-k), forward))
        if k <= behind:
            backward = moves.ctx_move(backward, lambda i: shifted(i, -1))
            found.append((source(k), backward))
    return found


def line_slots(length):
    arrivals = []
    for z in range(length):
        mine = []
        for k in range(1, length):
            pair = []
            if z + k < length:
                pair.append(("down", k, z + k))
            if z - k >= 0:
                pair.append(("up", k, z - k))
            if z >= length // 2:
                pair.reverse()
            mine += pair
        arrivals.append(mine)
    return [[arrivals[z][s] for z in range(length)] for s in range(length - 1)]


def line_gather(moves, block, z):
    length = moves.ctx // 2
    got = {("up", 0): block, ("down", 0): block}
    for k in range(1, length):
        got["up", k] = moves.ctx_move(
            got["up", k - 1], lambda i: i + 2 if k - 1 <= i // 2 < length - 1 else None
        )
        got["down", k] = moves.ctx_move(
            got["down", k - 1], lambda i: i - 2 if 0 < i // 2 <= length - k else None
        )
    blocks, places = [block], [np.arange(length, dtype=np.int32)]
    for slot in line_slots(length):
        choices = {}
        for place, (way, k, _) in enumerate(slot):
            choices.setdefault((way, k), []).append(place)
        value = None
        for key, where_z in choices.items():
            if value is None:
                value = got[key]
            else:
                here = functools.reduce(jnp.logical_or, [z == p for p in where_z])
                value = jnp.where(here, got[key], value)
        blocks.append(value)
        places.append(np.array([entry[2] for entry in slot], np.int32))
    return blocks, places


def butterfly(moves, value, merge):
    step = 1
    while step < moves.head:
        value = merge(value, moves.head_move(value, lambda h: h ^ step))
        step *= 2
    step = 1
    while step < moves.ctx:
        value = merge(value, moves.ctx_move(value, lambda i: i ^ step))
        step *= 2
    return value


def attention_kernel(count, heads, table, loc_ref, q_ref, *rest):
    sources, (o_ref, k_buf, v_buf, sems) = rest[:count], rest[count:]
    block = pl.program_id(0)
    span = k_buf.shape[1]
    rows = q_ref.shape[1]
    factor = HEAD_SIZE ** (-0.5) * math.log2(math.e)

    @pl.when(block == 0)
    def _():
        copies = []
        for n, source in enumerate(sources):
            for part, buf in enumerate((k_buf, v_buf)):
                copies.append(
                    pltpu.make_async_copy(source.at[part], buf.at[table[n]], sems.at[n, part])
                )
        for copy in copies:
            copy.start()
        for copy in copies:
            copy.wait()

    query = jnp.concatenate(
        [q_ref[0, :, n * HEAD_SIZE : (n + 1) * HEAD_SIZE] for n in range(heads)], axis=0
    )

    def attend(j, carry, masked):
        run_max, run_sum, run_acc = carry
        scores = lax.dot_general(
            query, k_buf[j], (((1,), (1,)), ((), ())), preferred_element_type=jnp.float32
        )
        if masked:
            row_pos = jnp.concatenate([loc_ref[0]] * heads, axis=0)
            key_pos = j * span + lax.broadcasted_iota(jnp.int32, scores.shape, 1)
            scores = jnp.where(key_pos <= row_pos, scores, neg_big)
        block_max = jnp.max(scores, axis=1, keepdims=True)
        weights = jnp.exp2((scores - block_max) * factor)
        block_sum = jnp.sum(weights, axis=1, keepdims=True)
        block_acc = jnp.dot(
            weights.astype(jnp.bfloat16), v_buf[j], preferred_element_type=jnp.float32
        )
        new_max = jnp.maximum(run_max, block_max)
        old = jnp.exp2((run_max - new_max) * factor)
        new = jnp.exp2((block_max - new_max) * factor)
        return new_max, run_sum * old + block_sum * new, run_acc * old + block_acc * new

    start = (
        jnp.full((rows * heads, 1), neg_big, jnp.float32),
        jnp.zeros((rows * heads, 1), jnp.float32),
        jnp.zeros((rows * heads, HEAD_SIZE), jnp.float32),
    )
    carry = lax.fori_loop(0, block, lambda j, c: attend(j, c, False), start)
    _, total, acc = attend(block, carry, True)
    out = (acc / total).astype(o_ref.dtype)
    for n in range(heads):
        o_ref[0, :, n * HEAD_SIZE : (n + 1) * HEAD_SIZE] = out[n * rows : (n + 1) * rows]


def attention(query, locations, blocks, table):
    row_blocks, rows, width = query.shape
    count, span = len(blocks), blocks[0].shape[1]
    heads = width // HEAD_SIZE
    pairs = row_blocks * (row_blocks + 1) // 2 * rows * heads * span
    return pl.pallas_call(
        functools.partial(attention_kernel, count, heads),
        out_shape=jax.ShapeDtypeStruct(query.shape, jnp.bfloat16),
        grid_spec=pltpu.PrefetchScalarGridSpec(
            num_scalar_prefetch=1,
            grid=(row_blocks,),
            in_specs=[
                pl.BlockSpec((1, rows, 1), lambda b, t: (b, 0, 0)),
                pl.BlockSpec((1, rows, width), lambda b, t: (b, 0, 0)),
            ]
            + [pl.BlockSpec(memory_space=pl.ANY)] * count,
            out_specs=pl.BlockSpec((1, rows, width), lambda b, t: (b, 0, 0)),
            scratch_shapes=[
                pltpu.VMEM((count, span, HEAD_SIZE), jnp.bfloat16),
                pltpu.VMEM((count, span, HEAD_SIZE), jnp.bfloat16),
                pltpu.SemaphoreType.DMA((count, 2)),
            ],
        ),
        compiler_params=pltpu.CompilerParams(
            dimension_semantics=("arbitrary",), vmem_limit_bytes=40 << 20
        ),
        cost_estimate=pl.CostEstimate(
            flops=4 * pairs * HEAD_SIZE,
            bytes_accessed=4 * count * span * HEAD_SIZE + 4 * query.size,
            transcendentals=pairs,
        ),
    )(table, locations, query, *blocks)


def exit_kernel(steps, final, info, scale_ref, gain_ref, own_ref, other_ref, lex_ref, *rest):
    rest = list(rest)
    before = rest.pop(0)
    if final:
        div_ref, token_ref, out_ref, normed, acc, stats = rest
    else:
        acc, normed = rest
    tile, k = pl.program_id(0), pl.program_id(1)
    rows = own_ref.shape[1]
    width = lex_ref.shape[1]

    @pl.when(tile == 0)
    def _():
        gain = gain_ref[0]
        for n, ref in enumerate((own_ref, other_ref)):
            wide = ref[0].astype(jnp.float32)
            part = scale_ref[info[steps + n]]
            normed[k, n * rows : (n + 1) * rows] = (wide * part * gain).astype(jnp.bfloat16)

    product = jnp.dot(normed[k], lex_ref[...], preferred_element_type=jnp.float32)

    @pl.when(k == 0)
    def _():
        acc[...] = (before[...] + product) if before is not None else product

    @pl.when(k > 0)
    def _():
        acc[...] += product

    if final:

        @pl.when((tile == 0) & (k == 0))
        def _():
            lane = lax.broadcasted_iota(jnp.int32, stats.shape, 1)
            stats[...] = jnp.where(lane == 0, neg_big, 0.0)

        @pl.when(k == steps - 1)
        def _():
            for n in range(2):
                part = slice(n * rows, (n + 1) * rows)
                which = info[steps + n]
                scaled = acc[part] * (1.0 / div_ref[which])
                column = (
                    info[steps + 2]
                    + tile * width
                    + lax.broadcasted_iota(jnp.int32, scaled.shape, 1)
                )
                found = jnp.sum(
                    jnp.where(column == token_ref[which], scaled, 0.0), axis=1, keepdims=True
                )
                top, total, picked = stats[part, 0:1], stats[part, 1:2], stats[part, 2:3]
                new_top = jnp.maximum(top, jnp.max(scaled, axis=1, keepdims=True))
                total = total * jnp.exp(top - new_top) + jnp.sum(
                    jnp.exp(scaled - new_top), axis=1, keepdims=True
                )
                lane = lax.broadcasted_iota(jnp.int32, (rows, stats.shape[1]), 1)
                stats[part] = jnp.where(
                    lane == 0, new_top, jnp.where(lane == 1, total, picked + found)
                )

        @pl.when((k == steps - 1) & (tile == pl.num_programs(0) - 1))
        def _():
            out_ref[...] = stats[...]


def exit_piece(info, scale, gain, own, other, lexicon, before, row_args=None):
    steps, rows, depth = own.shape
    width = lexicon.shape[1]
    tile = min(1024, width)
    final = row_args is not None
    whole = lambda a: pl.BlockSpec(a.shape, lambda n, k, i: (0,) * a.ndim)
    piece = pl.BlockSpec((1, rows, depth), lambda n, k, i: (jnp.where(n == 0, k, steps - 1), 0, 0))
    wide = pl.BlockSpec((2 * rows, tile), lambda n, k, i: (0, n))
    in_specs = [
        whole(scale),
        pl.BlockSpec((1, 1, depth), lambda n, k, i: (i[k], 0, 0)),
        piece,
        piece,
        pl.BlockSpec((depth, tile), lambda n, k, i: (i[k], n)),
    ]
    args = [info, scale, gain, own, other, lexicon]
    body = functools.partial(exit_kernel, steps, final)
    if before is not None:
        in_specs.append(wide)
        args.append(before)
    else:
        inner = body
        body = lambda *refs: inner(*refs[:6], None, *refs[6:])
    normed = pltpu.VMEM((steps, 2 * rows, depth), jnp.bfloat16)
    if final:
        in_specs += [whole(a) for a in row_args]
        args += list(row_args)
        out_shape = jax.ShapeDtypeStruct((2 * rows, 128), jnp.float32)
        out_specs = pl.BlockSpec((2 * rows, 128), lambda n, k, i: (0, 0))
        scratch = [
            normed,
            pltpu.VMEM((2 * rows, tile), jnp.float32),
            pltpu.VMEM((2 * rows, 128), jnp.float32),
        ]
    else:
        out_shape = jax.ShapeDtypeStruct((2 * rows, width), jnp.float32)
        out_specs = wide
        scratch = [normed]
    return pl.pallas_call(
        body,
        out_shape=out_shape,
        grid_spec=pltpu.PrefetchScalarGridSpec(
            num_scalar_prefetch=1,
            grid=(width // tile, steps),
            in_specs=in_specs,
            out_specs=out_specs,
            scratch_shapes=scratch,
        ),
        compiler_params=pltpu.CompilerParams(
            dimension_semantics=("arbitrary", "arbitrary"), vmem_limit_bytes=48 << 20
        ),
        cost_estimate=pl.CostEstimate(
            flops=4 * steps * rows * depth * width,
            bytes_accessed=2 * steps * depth * (width + 2 * rows),
            transcendentals=0,
        ),
    )(*args)


def shards(
    moves,
    probe_vectors,
    lookup_tensor,
    payload_tensor,
    sequence_locations,
    attention_return_matrix,
    skip_stream_state,
    early_rescaling_factor,
    lexicon_projection_matrix,
    calibrating_divisor,
    desired_tokens_list,
):
    ctx, head = moves.ctx, moves.head
    i, h = lax.axis_index("ctx"), lax.axis_index("head")
    rows_here, width_here = probe_vectors.shape
    heads_here = width_here // HEAD_SIZE
    total_rows = rows_here * ctx
    kv_here = lookup_tensor.shape[1] // HEAD_SIZE
    half = ctx // kv_here
    head_parts = min(ctx, heads_here)
    row_parts = ctx // head_parts
    part_rows, part_width = rows_here // row_parts, width_here // head_parts

    mine = i // half

    def of_head(which):
        start = which * HEAD_SIZE
        return jnp.stack(
            [
                lax.dynamic_slice_in_dim(a, start, HEAD_SIZE, 1)
                for a in (lookup_tensor, payload_tensor)
            ]
        )

    kept = [(np.arange(ctx, dtype=np.int32), of_head(mine))]
    for shift in range(1, kv_here):
        sent = of_head((mine + shift) % kv_here)
        came = moves.ctx_move(sent, lambda s: (s + shift * half) % ctx)
        kept.append((np.array([(s - shift * half) % ctx for s in range(ctx)], np.int32), came))
    blocks, tables = [], []
    for n, (origin, block) in enumerate(kept):
        long, short = half // 2, half - 1 - half // 2
        ahead, behind = (long, short) if n % 2 == 0 else (short, long)
        for source, got in ring_gather(moves, block, half, ahead, behind):
            blocks.append(got)
            tables.append(origin[source])
    table = jnp.asarray(np.stack(tables, 1))[i]

    pieces = probe_vectors.reshape(row_parts, part_rows, head_parts, part_width)
    pieces = pieces.transpose(2, 0, 1, 3).reshape(ctx, part_rows, part_width)
    query = lax.all_to_all(pieces, "ctx", split_axis=0, concat_axis=0, tiled=True)
    locations = sequence_locations.reshape(ctx, row_parts, part_rows)
    locations = lax.dynamic_index_in_dim(locations, i % row_parts, 1, keepdims=False)
    attn = attention(query, locations[..., None], blocks, table)

    if row_parts == 1:
        mixed_part = None
        for source, got in ring_gather(
            moves, attn.reshape(total_rows, part_width), ctx, ctx // 2, ctx - 1 - ctx // 2
        ):
            start = jnp.asarray(source)[i] * part_width
            matrix = lax.dynamic_slice_in_dim(attention_return_matrix, start, part_width, 0)
            term = jnp.dot(got, matrix, preferred_element_type=jnp.float32)
            mixed_part = term if mixed_part is None else mixed_part + term
    else:
        every = lax.all_gather(attn, "ctx").reshape(
            head_parts, row_parts, ctx, part_rows, part_width
        )
        every = every.transpose(2, 1, 3, 0, 4).reshape(total_rows, width_here)
        mixed_part = jnp.dot(every, attention_return_matrix, preferred_element_type=jnp.float32)

    y, core = h // 2, h % 2
    depth = mixed_part.shape[1]
    exit_rows = total_rows // head
    quarters = mixed_part.reshape(head // 2, 2, exit_rows, depth)
    keep = lax.dynamic_index_in_dim(quarters, core, 1, keepdims=False)
    give = lax.dynamic_index_in_dim(quarters, 1 - core, 1, keepdims=False)
    both = keep + moves.core_swap(give)
    mixed_rows = lax.dynamic_index_in_dim(both, y, 0, keepdims=False) + moves.y_swap(
        lax.dynamic_index_in_dim(both, 1 - y, 0, keepdims=False)
    )
    hidden = (skip_stream_state.astype(jnp.float32) + mixed_rows).astype(jnp.bfloat16)

    widened = hidden.astype(jnp.float32)
    squares = jnp.zeros((head, exit_rows), jnp.float32)
    squares = lax.dynamic_update_slice(squares, jnp.sum(widened * widened, axis=1)[None], (h, 0))
    squares = butterfly(moves, squares, jnp.add)
    scale = lax.rsqrt(squares / (depth * ctx) + eps)[..., None]
    gain = lax.all_gather(early_rescaling_factor, "ctx").reshape(ctx, 1, depth)

    z = i // 2
    line, places = line_gather(moves, hidden, z)
    across = [moves.minor_swap(b) for b in line]
    beside = [moves.y_swap(b) for b in line]
    line, across, beside = (jnp.stack(b) for b in (line, across, beside))
    cut = exit_rows // 2
    diagonal = jnp.concatenate(
        [moves.y_swap(across[:, :cut]), moves.minor_swap(beside[:, cut:])], axis=1
    )

    vocab_here = lexicon_projection_matrix.shape[1]
    offset = (i * head + h) * vocab_here
    line_place = jnp.asarray(np.stack(places, 1))[z]
    row_args = (
        calibrating_divisor.reshape(head, exit_rows, 1),
        desired_tokens_list.reshape(head, exit_rows, 1),
    )

    def piece(stack, minor, y_of, before, args):
        rows_of = y_of * 2 + core
        info = jnp.concatenate(
            [line_place * 2 + minor, jnp.stack([rows_of, rows_of ^ 1, offset])]
        ).astype(jnp.int32)
        other = moves.core_swap(stack)
        return exit_piece(info, scale, gain, stack, other, lexicon_projection_matrix, before, args)

    minor = i % 2
    near = piece(line, minor, y, None, None)
    near = piece(across, 1 - minor, y, near, row_args)
    far = piece(beside, minor, 1 - y, None, None)
    far = piece(diagonal, 1 - minor, 1 - y, far, row_args)

    def in_order(pair, second):
        return jnp.where(second == 0, pair, pair[::-1])

    stats = jnp.stack([near, far])[:, :, :3].reshape(2, 2, exit_rows, 3)
    stats = in_order(stats, y)
    stats = jnp.where(core == 0, stats, stats[:, ::-1])
    stats = stats.reshape(total_rows, 3).T.reshape(3, total_rows)

    def merge(a, b):
        top = jnp.maximum(a[0], b[0])
        total = a[1] * jnp.exp(a[0] - top) + b[1] * jnp.exp(b[0] - top)
        return jnp.stack([top, total, a[2] + b[2]])

    peak, total, picked = butterfly(moves, stats, merge)
    return hidden, picked - peak - jnp.log(total)


def solution(mesh):
    placed = (
        P("ctx", "head"),
        P("ctx", "head"),
        P("ctx", "head"),
        P(),
        P("head", "ctx"),
        P("head", "ctx"),
        P("ctx"),
        P(None, ("ctx", "head")),
        P(),
        P(),
    )
    return jax.shard_map(
        functools.partial(shards, Moves(mesh)),
        mesh=mesh,
        in_specs=placed,
        out_specs=(P("head", "ctx"), P()),
        check_vma=False,
    )
```

time: 879 us -> 458 us (0.52)
  waiting for transfers between devices: 560 us -> 216 us
  matrix products: 131 us -> 18.1 us
  blocking collectives: 136 us -> 30.6 us
  Pallas kernels: 0 us -> 102 us
  starting transfers between devices: 0.51 us -> 54.7 us
  other arithmetic: 29.8 us -> 10.8 us
  local copies, waits for them, and re-layouts: 7.37 us -> 18.6 us
    all_gather x4 -> x0, waiting for transfers between devices: 322 us -> none  [the longest x1 106 us: shards(): lax.all_gather(full_rows, 'head', axis=0, tiled=True)]
    reduce_scatter x3 -> x0, waiting for transfers between devices: 237 us -> none  [the longest x1 151 us: shards(): lax.psum_scatter(local_acc * rescale[..., None], 'ctx', scatter_dimension...]
    ppermute x0 -> x46, waiting for transfers between devices: none -> 216 us  [the longest x31 153 us: ctx_move(): return lax.ppermute(value, AXES, self.perm(ctx_to=ctx_to))]
    dot_general x10 -> x8, matrix products: 131 us -> 18.1 us  [shards(): term = jnp.dot(got, matrix, preferred_element_type=jnp.float32)]
    pallas_call x0 -> x5, Pallas kernels: none -> 102 us  [the longest x4 74.4 us: exit_piece(): pl.pallas_call(body, out_shape=out_shape, grid_spec=pltpu.PrefetchScalarG...]
    pmax x2 -> x0, blocking collectives: 73.8 us -> none  [the longest x1 39.5 us: shards(): peak = lax.pmax(local_peak, ('ctx', 'head'))]
    psum x2 -> x0, blocking collectives: 62.4 us -> none  [the longest x1 41 us: shards(): lax.psum((jnp.sum(jnp.exp(tempered_affinities - peak[:, None]), axis=1),...]
    ppermute x0 -> x46, starting transfers between devices: none -> 50 us  [the longest x31 37.4 us: ctx_move(): return lax.ppermute(value, AXES, self.perm(ctx_to=ctx_to))]
  transfers between devices with their start and end apart: 7 -> 47, of which waited for: 7 -> 29; matrix products, arithmetic and copies ran while one was open for 1% -> 7% of each run, Pallas kernels for 0% -> 12%
where the time goes in v1:
time: 458 us; the launch traced here: 457 us
  waiting for transfers between devices  216 us (47%)
  Pallas kernels  102 us (22%)
  starting transfers between devices  54.7 us (12%)
  blocking collectives  30.6 us (7%)
  local copies, waits for them, and re-layouts  18.6 us (4%)
  matrix products  18.1 us (4%)
  other arithmetic  10.8 us (2%)
  between operations  5.71 us (1%)
    ppermute x31, waiting for transfers between devices, ctx_move(): return lax.ppermute(value, AXES, self.perm(ctx_to=ctx_to))  153 us
    pallas_call x4, Pallas kernels, exit_piece(): pl.pallas_call(body, out_shape=out_shape, grid_spec=pltpu.PrefetchScalarG...  74.4 us
    ppermute x15, waiting for transfers between devices, head_move(): return lax.ppermute(value, AXES, self.perm(head_to=head_to))  63.2 us
    ppermute x31, starting transfers between devices, ctx_move(): return lax.ppermute(value, AXES, self.perm(ctx_to=ctx_to))  37.4 us
    all_gather x1, blocking collectives, shards(): gain = lax.all_gather(early_rescaling_factor, 'ctx').reshape(ctx, 1, depth)  30.6 us
    pallas_call x1, Pallas kernels, attention(): pl.pallas_call(functools.partial(attention_kernel, count, heads), out_sha...  27.2 us
    dot_general x8, matrix products, shards(): term = jnp.dot(got, matrix, preferred_element_type=jnp.float32)  18.1 us
    ppermute x15, starting transfers between devices, head_move(): return lax.ppermute(value, AXES, self.perm(head_to=head_to))  12.6 us
  transfers between devices with their start and end apart: 47, of which 29 were waited for; matrix products, arithmetic and copies ran while one was open for 7% of the time, Pallas kernels for 12%

profile of v1, /device:TPU:0, one launch (start us, length us, event | category | flops | bytes accessed | tf_op | source)
XLA Modules:
  0.0 456.6 jit_solution(4771729994751083668)
XLA Ops:
  2.1 4.1 collective-permute-start.3
  7.9 21.5 %collective-permute-done.3.rest_4_ = bf16[2,1024,128]{2,1,0:T(8,128)(2,1)S(1)} collective-permute-done((bf16[2,1024,128]{2,1,0:T(8,128)(2,1)S(1)}, bf16[2,1024,128]{2,1,0:T(8,128)(2,1)S(1)}, u32[]{:S(2)}, u32[]{:S(2)}) %collective-permute-start.3) | collective-permute-done | bytes 524320 | tf_op jit(solution)/shard_map/ppermute | solution.py:36
  32.3 4.7 %all-to-all-start = ((bf16[8,128,256]{2,1,0:T(8,128)(2,1)}), bf16[8,128,256]{2,1,0:T(8,128)(2,1)S(1)}, u32[]{:S(2)}, u32[]{:S(2)}) async-start(bf16[8,128,256]{2,1,0:T(8,128)(2,1)} %bitcast.4), calls=%async_computation | async-start | bytes 1048576 | tf_op jit(solution)/shard_map/all_to_all | solution.py:399
  37.0 2.0 collective-permute-start.1
  39.0 2.0 collective-permute-start.2
  41.0 7.2 %collective-permute-done.5.rest_6_ = bf16[2,1024,128]{2,1,0:T(8,128)(2,1)S(1)} collective-permute-done((bf16[2,1024,128]{2,1,0:T(8,128)(2,1)S(1)}, bf16[2,1024,128]{2,1,0:T(8,128)(2,1)S(1)}, u32[]{:S(2)}, u32[]{:S(2)}) %collective-permute-start.5) | collective-permute-done | bytes 524320 | tf_op jit(solution)/shard_map/ppermute | solution.py:36
  49.6 14.3 %collective-permute-done.1.rest_2_ = bf16[2,1024,128]{2,1,0:T(8,128)(2,1)} collective-permute-done((bf16[2,1024,128]{2,1,0:T(8,128)(2,1)S(1)}, bf16[2,1024,128]{2,1,0:T(8,128)(2,1)}, u32[]{:S(2)}, u32[]{:S(2)}) %collective-permute-start.1) | collective-permute-done | bytes 524320 | tf_op jit(solution)/shard_map/ppermute | solution.py:36
  63.9 4.1 collective-permute-done.2.rest_3_
  68.0 5.5 %collective-permute-done.6.rest_7_ = bf16[2,1024,128]{2,1,0:T(8,128)(2,1)} collective-permute-done((bf16[2,1024,128]{2,1,0:T(8,128)(2,1)S(1)}, bf16[2,1024,128]{2,1,0:T(8,128)(2,1)}, u32[]{:S(2)}, u32[]{:S(2)}) %collective-permute-start.6) | collective-permute-done | bytes 524320 | tf_op jit(solution)/shard_map/ppermute | solution.py:36
  74.5 27.2 %shard_map.203 = bf16[8,128,256]{2,1,0:T(8,128)(2,1)S(1)} custom-call(s32[8]{0:T(128)S(1)} %fusion.34.table, s32[8,128,1]{2,1,0:T(8,128)S(1)} %copy.36.loc_ref, bf16[8,128,256]{2,1,0:T(8,128)(2,1)S(1)} %all-to-all-done.q_ref, bf16[2,1024,128]{2,1,0:T(8,128)(2,1)S(1)} %pad_maximum_fusion.4.rest_0_, bf16[2,1024,128]{2,1,0:T(8,128)(2,1)S(1)} %collective-permute-done.rest_1_, ...), custom_call_target="tpu_custom_call" | custom-call | flops 4831838208 | bytes 5242880 | tf_op jit(solution)/shard_map/pallas_call | solution.py:195
  101.8 2.0 collective-permute-start.8
  112.6 1.9 fusion.15
  114.5 1.7 collective-permute-start.9
  118.2 8.6 %collective-permute-done.9 = bf16[1024,256]{1,0:T(8,128)(2,1)S(1)} collective-permute-done((bf16[1024,256]{1,0:T(8,128)(2,1)S(1)}, bf16[1024,256]{1,0:T(8,128)(2,1)S(1)}, u32[]{:S(2)}, u32[]{:S(2)}) %collective-permute-start.9) | collective-permute-done | bytes 524320 | tf_op jit(solution)/shard_map/ppermute | solution.py:36
  126.7 2.5 collective-permute-start.11
  130.9 8.0 %collective-permute-done.11 = bf16[1024,256]{1,0:T(8,128)(2,1)S(1)} collective-permute-done((bf16[1024,256]{1,0:T(8,128)(2,1)S(1)}, bf16[1024,256]{1,0:T(8,128)(2,1)S(1)}, u32[]{:S(2)}, u32[]{:S(2)}) %collective-permute-start.11) | collective-permute-done | bytes 524320 | tf_op jit(solution)/shard_map/ppermute | solution.py:36
  138.8 2.5 collective-permute-start.13
  141.3 2.7 fusion.5
  144.0 2.7 fusion.3
  146.7 3.6 collective-permute-done.13
  150.3 7.9 %add_add_fusion = f32[1024,1024]{1,0:T(8,128)} fusion(f32[1024,1024]{1,0:T(8,128)} %fusion.3, f32[1024,1024]{1,0:T(8,128)} %fusion.5, f32[1024,1024]{1,0:T(8,128)S(1)} %fusion.7, f32[1024,1024]{1,0:T(8,128)S(1)} %fusion.9, f32[1024,1024]{1,0:T(8,128)S(1)} %fusion.11, f32[1024,1024]{1,0:T(8,128)S(1)} %fusion.15, f32[1024,1024]{1,0:T(8,128)S(1)} %fusion.13, ...), kind=kOutput, calls=%fused_computation | convolution fusion | flops 544210944 | bytes 34603012 | tf_op jit(solution)/shard_map/dot_general | solution.py:411
  158.2 1.7 dynamic-slice_bitcast_fusion
  160.1 4.2 collective-permute-done.14
  164.3 2.6 bitcast_add_fusion
  168.7 23.7 %collective-permute-done.15 = f32[256,1024]{1,0:T(8,128)} collective-permute-done((f32[256,1024]{1,0:T(8,128)S(1)}, f32[256,1024]{1,0:T(8,128)}, u32[]{:S(2)}, u32[]{:S(2)}) %collective-permute-start.15) | collective-permute-done | bytes 1048608 | tf_op jit(solution)/shard_map/ppermute | solution.py:39
  194.1 4.3 collective-permute-start.22
  199.6 9.3 %collective-permute-done.22 = bf16[256,1024]{1,0:T(8,128)(2,1)S(1)} collective-permute-done((bf16[256,1024]{1,0:T(8,128)(2,1)S(1)}, bf16[256,1024]{1,0:T(8,128)(2,1)S(1)}, u32[]{:S(2)}, u32[]{:S(2)}) %collective-permute-start.22) | collective-permute-done | bytes 524320 | tf_op jit(solution)/shard_map/ppermute | solution.py:36
  209.6 3.5 collective-permute-done.23
  215.2 11.7 %collective-permute-done.26 = bf16[256,1024]{1,0:T(8,128)(2,1)S(1)} collective-permute-done((bf16[256,1024]{1,0:T(8,128)(2,1)S(1)}, bf16[256,1024]{1,0:T(8,128)(2,1)S(1)}, u32[]{:S(2)}, u32[]{:S(2)}) %collective-permute-start.26) | collective-permute-done | bytes 524320 | tf_op jit(solution)/shard_map/ppermute | solution.py:36
  229.4 10.6 %collective-permute-done.29 = bf16[256,1024]{1,0:T(8,128)(2,1)} collective-permute-done((bf16[256,1024]{1,0:T(8,128)(2,1)S(1)}, bf16[256,1024]{1,0:T(8,128)(2,1)}, u32[]{:S(2)}, u32[]{:S(2)}) %collective-permute-start.29) | collective-permute-done | bytes 524320 | tf_op jit(solution)/shard_map/ppermute | solution.py:36
  247.7 8.4 %collective-permute-done.24 = bf16[256,1024]{1,0:T(8,128)(2,1)S(1)} collective-permute-done((bf16[256,1024]{1,0:T(8,128)(2,1)S(1)}, bf16[256,1024]{1,0:T(8,128)(2,1)S(1)}, u32[]{:S(2)}, u32[]{:S(2)}) %collective-permute-start.24) | collective-permute-done | bytes 524320 | tf_op jit(solution)/shard_map/ppermute | solution.py:36
  257.6 9.7 %collective-permute-done.27 = bf16[256,1024]{1,0:T(8,128)(2,1)S(1)} collective-permute-done((bf16[256,1024]{1,0:T(8,128)(2,1)S(1)}, bf16[256,1024]{1,0:T(8,128)(2,1)S(1)}, u32[]{:S(2)}, u32[]{:S(2)}) %collective-permute-start.27) | collective-permute-done | bytes 524320 | tf_op jit(solution)/shard_map/ppermute | solution.py:36
  268.9 5.2 %collective-permute-done.30 = bf16[256,1024]{1,0:T(8,128)(2,1)S(1)} collective-permute-done((bf16[256,1024]{1,0:T(8,128)(2,1)S(1)}, bf16[256,1024]{1,0:T(8,128)(2,1)S(1)}, u32[]{:S(2)}, u32[]{:S(2)}) %collective-permute-start.30) | collective-permute-done | bytes 524320 | tf_op jit(solution)/shard_map/ppermute | solution.py:36
  277.5 6.0 %collective-permute-done.36 = bf16[256,1024]{1,0:T(8,128)(2,1)S(1)} collective-permute-done((bf16[256,1024]{1,0:T(8,128)(2,1)S(1)}, bf16[256,1024]{1,0:T(8,128)(2,1)S(1)}, u32[]{:S(2)}, u32[]{:S(2)}) %collective-permute-start.36) | collective-permute-done | bytes 524320 | tf_op jit(solution)/shard_map/ppermute | solution.py:39
  283.4 11.2 %collective-permute-done.37 = bf16[256,1024]{1,0:T(8,128)(2,1)S(1)} collective-permute-done((bf16[256,1024]{1,0:T(8,128)(2,1)S(1)}, bf16[256,1024]{1,0:T(8,128)(2,1)S(1)}, u32[]{:S(2)}, u32[]{:S(2)}) %collective-permute-start.37) | collective-permute-done | bytes 524320 | tf_op jit(solution)/shard_map/ppermute | solution.py:39
  296.2 2.3 slice.91
  303.1 13.7 %collective-permute-done.17 = f32[4,256]{1,0:T(4,128)S(1)} collective-permute-done((f32[4,256]{1,0:T(4,128)S(1)}, f32[4,256]{1,0:T(4,128)S(1)}, u32[]{:S(2)}, u32[]{:S(2)}) %collective-permute-start.17) | collective-permute-done | bytes 4128 | tf_op jit(solution)/shard_map/ppermute | solution.py:39
  317.7 6.7 %collective-permute-done.18 = f32[4,256]{1,0:T(4,128)S(1)} collective-permute-done((f32[4,256]{1,0:T(4,128)S(1)}, f32[4,256]{1,0:T(4,128)S(1)}, u32[]{:S(2)}, u32[]{:S(2)}) %collective-permute-start.18) | collective-permute-done | bytes 4128 | tf_op jit(solution)/shard_map/ppermute | solution.py:36
  324.7 3.4 collective-permute-done.19
  328.1 30.6 %all-gather = f32[8192]{0:T(1024)S(1)} all-gather(f32[1024]{0:T(1024)S(1)} %copy-done.9), channel_id=2, replica_groups=mesh['ctx'=8,'head'=4] {'ctx'}, dimensions={0}, use_global_device_ids=true | all-gather | bytes 36864 | tf_op jit(solution)/shard_map/all_gather | solution.py:437
  363.6 18.1 %shard_map.204.rest_0_ = f32[512,2048]{1,0:T(8,128)} custom-call(s32[7]{0:T(128)S(1)} %get-tuple-element.38.refs_0_, f32[4,256,1]{2,1,0:T(8,128)S(1)} %copy.38.refs_1_.scale_ref, f32[8,1,1024]{2,1,0:T(1,128)S(1)} %bitcast.93, bf16[4,256,1024]{2,1,0:T(8,128)(2,1)} %pad_maximum_fusion.1.refs_3_, bf16[4,256,1024]{2,1,0:T(8,128)(2,1)} %collective-permute-done.32.refs_4_, ...), custom_call_target="tpu_custom_call" | custom-call | flops 8589934592 | bytes 20971520 | tf_op jit(solution)/shard_map/pallas_call | solution.py:327
  381.7 18.0 %shard_map.206.rest_0_ = f32[512,2048]{1,0:T(8,128)} custom-call(s32[7]{0:T(128)S(1)} %get-tuple-element.39.refs_0_, f32[4,256,1]{2,1,0:T(8,128)S(1)} %copy.38.refs_1_.scale_ref, f32[8,1,1024]{2,1,0:T(1,128)S(1)} %bitcast.94, bf16[4,256,1024]{2,1,0:T(8,128)(2,1)} %pad_maximum_fusion.2.refs_3_, bf16[4,256,1024]{2,1,0:T(8,128)(2,1)} %collective-permute-done.40.refs_4_, ...), custom_call_target="tpu_custom_call" | custom-call | flops 8589934592 | bytes 20971520 | tf_op jit(solution)/shard_map/pallas_call | solution.py:327
  399.7 19.3 %shard_map.205 = f32[512,128]{1,0:T(8,128)S(1)} custom-call(s32[7]{0:T(128)S(1)} %get-tuple-element.40.info, f32[4,256,1]{2,1,0:T(8,128)S(1)} %copy.38.refs_1_.scale_ref, f32[8,1,1024]{2,1,0:T(1,128)S(1)} %bitcast.95, bf16[4,256,1024]{2,1,0:T(8,128)(2,1)S(1)} %pad_maximum_fusion.own_ref, bf16[4,256,1024]{2,1,0:T(8,128)(2,1)} %collective-permute-done.31.other_ref, ...), custom_call_target="tpu_custom_call" | custom-call | flops 8589934592 | bytes 20971520 | tf_op jit(solution)/shard_map/pallas_call | solution.py:327
  419.0 19.0 %shard_map.207 = f32[512,128]{1,0:T(8,128)S(1)} custom-call(s32[7]{0:T(128)S(1)} %get-tuple-element.41.info, f32[4,256,1]{2,1,0:T(8,128)S(1)} %copy.38.refs_1_.scale_ref, f32[8,1,1024]{2,1,0:T(1,128)S(1)} %bitcast.96, bf16[4,256,1024]{2,1,0:T(8,128)(2,1)S(1)} %constant_dynamic-update-slice_fusion.own_ref, ...), custom_call_target="tpu_custom_call" | custom-call | flops 8589934592 | bytes 20971520 | tf_op jit(solution)/shard_map/pallas_call | solution.py:327
  441.3 2.2 collective-permute-done.42
  443.9 3.4 collective-permute-done.43
  447.4 3.7 collective-permute-done.44
  451.4 4.5 collective-permute-done.45
  (148 shorter events, 57.2 us)
Async XLA Ops:
  2.1 27.3 %collective-permute-start.3 = (bf16[2,1024,128]{2,1,0:T(8,128)(2,1)S(1)}, bf16[2,1024,128]{2,1,0:T(8,128)(2,1)S(1)}, u32[]{:S(2)}, u32[]{:S(2)}) collective-permute-start(bf16[2,1024,128]{2,1,0:T(8,128)(2,1)S(1)} %pad_maximum_fusion.5), channel_id=1, source_target_pairs={{0,16},{1,17},{2,18},{3,19},{4,20},{5,21},{6,22},{7,23},{8,24},{9,... | collective-permute-start | bytes 1572872 | tf_op jit(solution)/shard_map/ppermute | solution.py:36
  6.2 32.8 %collective-permute-start = (bf16[2,1024,128]{2,1,0:T(8,128)(2,1)S(1)}, bf16[2,1024,128]{2,1,0:T(8,128)(2,1)S(1)}, u32[]{:S(2)}, u32[]{:S(2)}) collective-permute-start(bf16[2,1024,128]{2,1,0:T(8,128)(2,1)S(1)} %pad_maximum_fusion.4.rest_0_), channel_id=1, source_target_pairs={{0,8},{1,9},{2,10},{3,11},{4,0},{5,1},{6,2},{7,3},{8,12},{9,13},{1... | collective-permute-start | bytes 1572872 | tf_op jit(solution)/shard_map/ppermute | solution.py:36
  29.4 18.9 %collective-permute-start.5 = (bf16[2,1024,128]{2,1,0:T(8,128)(2,1)S(1)}, bf16[2,1024,128]{2,1,0:T(8,128)(2,1)S(1)}, u32[]{:S(2)}, u32[]{:S(2)}) collective-permute-start(bf16[2,1024,128]{2,1,0:T(8,128)(2,1)S(1)} %collective-permute-done.3.rest_4_), channel_id=1, source_target_pairs={{0,4},{1,5},{2,6},{3,7},{4,12},{5,13},{6,14},{7,15},{8,0},{9,1},{1... | collective-permute-start | bytes 1572872 | tf_op jit(solution)/shard_map/ppermute | solution.py:36
  32.3 31.6 %all-to-all-start = ((bf16[8,128,256]{2,1,0:T(8,128)(2,1)}), bf16[8,128,256]{2,1,0:T(8,128)(2,1)S(1)}, u32[]{:S(2)}, u32[]{:S(2)}) async-start(bf16[8,128,256]{2,1,0:T(8,128)(2,1)} %bitcast.4), calls=%async_computation | async-start | bytes 1048576 | tf_op jit(solution)/shard_map/all_to_all | solution.py:399
  37.0 27.0 %collective-permute-start.1 = (bf16[2,1024,128]{2,1,0:T(8,128)(2,1)S(1)}, bf16[2,1024,128]{2,1,0:T(8,128)(2,1)}, u32[]{:S(2)}, u32[]{:S(2)}) collective-permute-start(bf16[2,1024,128]{2,1,0:T(8,128)(2,1)S(1)} %pad_maximum_fusion.4.rest_0_), channel_id=1, source_target_pairs={{0,4},{1,5},{2,6},{3,7},{4,12},{5,13},{6,14},{7,15},{8,0},{9,1},{1... | collective-permute-start | bytes 1572872 | tf_op jit(solution)/shard_map/ppermute | solution.py:36
  39.0 24.9 %collective-permute-start.4 = (bf16[2,1024,128]{2,1,0:T(8,128)(2,1)S(1)}, bf16[2,1024,128]{2,1,0:T(8,128)(2,1)}, u32[]{:S(2)}, u32[]{:S(2)}) collective-permute-start(bf16[2,1024,128]{2,1,0:T(8,128)(2,1)S(1)} %collective-permute-done.3.rest_4_), channel_id=1, source_target_pairs={{0,8},{1,9},{2,10},{3,11},{4,0},{5,1},{6,2},{7,3},{8,12},{9,13},{1... | collective-permute-start | bytes 1572872 | tf_op jit(solution)/shard_map/ppermute | solution.py:36
  39.0 29.0 %collective-permute-start.2 = (bf16[2,1024,128]{2,1,0:T(8,128)(2,1)S(1)}, bf16[2,1024,128]{2,1,0:T(8,128)(2,1)}, u32[]{:S(2)}, u32[]{:S(2)}) collective-permute-start(bf16[2,1024,128]{2,1,0:T(8,128)(2,1)S(1)} %collective-permute-done.rest_1_), channel_id=1, source_target_pairs={{0,8},{1,9},{2,10},{3,11},{4,0},{5,1},{6,2},{7,3},{8,12},{9,13},{1... | collective-permute-start | bytes 1572872 | tf_op jit(solution)/shard_map/ppermute | solution.py:36
  48.2 25.2 %collective-permute-start.6 = (bf16[2,1024,128]{2,1,0:T(8,128)(2,1)S(1)}, bf16[2,1024,128]{2,1,0:T(8,128)(2,1)}, u32[]{:S(2)}, u32[]{:S(2)}) collective-permute-start(bf16[2,1024,128]{2,1,0:T(8,128)(2,1)S(1)} %collective-permute-done.5.rest_6_), channel_id=1, source_target_pairs={{0,4},{1,5},{2,6},{3,7},{4,12},{5,13},{6,14},{7,15},{8,0},{9,1},{1... | collective-permute-start | bytes 1572872 | tf_op jit(solution)/shard_map/ppermute | solution.py:36
  101.7 12.8 %collective-permute-start.7 = (bf16[1024,256]{1,0:T(8,128)(2,1)S(1)}, bf16[1024,256]{1,0:T(8,128)(2,1)S(1)}, u32[]{:S(2)}, u32[]{:S(2)}) collective-permute-start(bf16[1024,256]{1,0:T(8,128)(2,1)S(1)} %bitcast.88), channel_id=1, source_target_pairs={{0,8},{1,9},{2,10},{3,11},{4,0},{5,1},{6,2},{7,3},{8,16},{9,17},{1... | collective-permute-start | bytes 1572872 | tf_op jit(solution)/shard_map/ppermute | solution.py:36
  101.8 14.9 %collective-permute-start.8 = (bf16[1024,256]{1,0:T(8,128)(2,1)S(1)}, bf16[1024,256]{1,0:T(8,128)(2,1)S(1)}, u32[]{:S(2)}, u32[]{:S(2)}) collective-permute-start(bf16[1024,256]{1,0:T(8,128)(2,1)S(1)} %bitcast.89), channel_id=1, source_target_pairs={{0,4},{1,5},{2,6},{3,7},{4,12},{5,13},{6,14},{7,15},{8,0},{9,1},{1... | collective-permute-start | bytes 1572872 | tf_op jit(solution)/shard_map/ppermute | solution.py:36
  114.5 12.2 %collective-permute-start.9 = (bf16[1024,256]{1,0:T(8,128)(2,1)S(1)}, bf16[1024,256]{1,0:T(8,128)(2,1)S(1)}, u32[]{:S(2)}, u32[]{:S(2)}) collective-permute-start(bf16[1024,256]{1,0:T(8,128)(2,1)S(1)} %collective-permute-done.7), channel_id=1, source_target_pairs={{0,8},{1,9},{2,10},{3,11},{4,0},{5,1},{6,2},{7,3},{8,16},{9,17},{1... | collective-permute-start | bytes 1572872 | tf_op jit(solution)/shard_map/ppermute | solution.py:36
  116.7 12.5 %collective-permute-start.10 = (bf16[1024,256]{1,0:T(8,128)(2,1)S(1)}, bf16[1024,256]{1,0:T(8,128)(2,1)S(1)}, u32[]{:S(2)}, u32[]{:S(2)}) collective-permute-start(bf16[1024,256]{1,0:T(8,128)(2,1)S(1)} %collective-permute-done.8), channel_id=1, source_target_pairs={{0,4},{1,5},{2,6},{3,7},{4,12},{5,13},{6,14},{7,15},{8,0},{9,1},{1... | collective-permute-start | bytes 1572872 | tf_op jit(solution)/shard_map/ppermute | solution.py:36
  126.7 12.1 %collective-permute-start.11 = (bf16[1024,256]{1,0:T(8,128)(2,1)S(1)}, bf16[1024,256]{1,0:T(8,128)(2,1)S(1)}, u32[]{:S(2)}, u32[]{:S(2)}) collective-permute-start(bf16[1024,256]{1,0:T(8,128)(2,1)S(1)} %collective-permute-done.9), channel_id=1, source_target_pairs={{0,8},{1,9},{2,10},{3,11},{4,0},{5,1},{6,2},{7,3},{8,16},{9,17},{1... | collective-permute-start | bytes 1572872 | tf_op jit(solution)/shard_map/ppermute | solution.py:36
  129.2 14.8 %collective-permute-start.12 = (bf16[1024,256]{1,0:T(8,128)(2,1)S(1)}, bf16[1024,256]{1,0:T(8,128)(2,1)S(1)}, u32[]{:S(2)}, u32[]{:S(2)}) collective-permute-start(bf16[1024,256]{1,0:T(8,128)(2,1)S(1)} %collective-permute-done.10), channel_id=1, source_target_pairs={{0,4},{1,5},{2,6},{3,7},{4,12},{5,13},{6,14},{7,15},{8,0},{9,1},{1... | collective-permute-start | bytes 1572872 | tf_op jit(solution)/shard_map/ppermute | solution.py:36
  138.8 11.5 %collective-permute-start.13 = (bf16[1024,256]{1,0:T(8,128)(2,1)S(1)}, bf16[1024,256]{1,0:T(8,128)(2,1)}, u32[]{:S(2)}, u32[]{:S(2)}) collective-permute-start(bf16[1024,256]{1,0:T(8,128)(2,1)S(1)} %collective-permute-done.11), channel_id=1, source_target_pairs={{0,8},{1,9},{2,10},{3,11},{4,0},{5,1},{6,2},{7,3},{8,16},{9,17},{1... | collective-permute-start | bytes 1572872 | tf_op jit(solution)/shard_map/ppermute | solution.py:36
  160.0 4.4 collective-permute-start.14
  167.1 25.4 %collective-permute-start.15 = (f32[256,1024]{1,0:T(8,128)S(1)}, f32[256,1024]{1,0:T(8,128)}, u32[]{:S(2)}, u32[]{:S(2)}) collective-permute-start(f32[256,1024]{1,0:T(8,128)S(1)} %dynamic-slice_bitcast_fusion.1), channel_id=1, source_target_pairs={{0,2},{1,3},{2,0},{3,1},{4,6},{5,7},{6,4},{7,5},{8,10},{9,11},{10,... | collective-permute-start | bytes 3145736 | tf_op jit(solution)/shard_map/ppermute | solution.py:39
  194.1 14.9 %collective-permute-start.22 = (bf16[256,1024]{1,0:T(8,128)(2,1)S(1)}, bf16[256,1024]{1,0:T(8,128)(2,1)S(1)}, u32[]{:S(2)}, u32[]{:S(2)}) collective-permute-start(bf16[256,1024]{1,0:T(8,128)(2,1)S(1)} %get-tuple-element.9), channel_id=1, source_target_pairs={{0,8},{1,9},{2,10},{3,11},{4,12},{5,13},{6,14},{7,15},{8,16},{9,17... | collective-permute-start | bytes 1572872 | tf_op jit(solution)/shard_map/ppermute | solution.py:36
  198.3 14.7 %collective-permute-start.23 = (bf16[256,1024]{1,0:T(8,128)(2,1)S(1)}, bf16[256,1024]{1,0:T(8,128)(2,1)S(1)}, u32[]{:S(2)}, u32[]{:S(2)}) collective-permute-start(bf16[256,1024]{1,0:T(8,128)(2,1)S(1)} %get-tuple-element.9), channel_id=1, source_target_pairs={{8,0},{9,1},{10,2},{11,3},{12,4},{13,5},{14,6},{15,7},{16,8},{17,9... | collective-permute-start | bytes 1572872 | tf_op jit(solution)/shard_map/ppermute | solution.py:36
  208.9 5.4 %collective-permute-start.25 = (bf16[256,1024]{1,0:T(8,128)(2,1)S(1)}, bf16[256,1024]{1,0:T(8,128)(2,1)S(1)}, u32[]{:S(2)}, u32[]{:S(2)}) collective-permute-start(bf16[256,1024]{1,0:T(8,128)(2,1)S(1)} %collective-permute-done.22), channel_id=1, source_target_pairs={{8,16},{9,17},{10,18},{11,19},{12,20},{13,21},{14,22},{15,23},{16,... | collective-permute-start | bytes 1572872 | tf_op jit(solution)/shard_map/ppermute | solution.py:36
  213.1 13.9 %collective-permute-start.26 = (bf16[256,1024]{1,0:T(8,128)(2,1)S(1)}, bf16[256,1024]{1,0:T(8,128)(2,1)S(1)}, u32[]{:S(2)}, u32[]{:S(2)}) collective-permute-start(bf16[256,1024]{1,0:T(8,128)(2,1)S(1)} %collective-permute-done.23), channel_id=1, source_target_pairs={{8,0},{9,1},{10,2},{11,3},{12,4},{13,5},{14,6},{15,7},{16,8},{17,9... | collective-permute-start | bytes 1572872 | tf_op jit(solution)/shard_map/ppermute | solution.py:36
  214.4 15.1 %collective-permute-start.28 = (bf16[256,1024]{1,0:T(8,128)(2,1)S(1)}, bf16[256,1024]{1,0:T(8,128)(2,1)S(1)}, u32[]{:S(2)}, u32[]{:S(2)}) collective-permute-start(bf16[256,1024]{1,0:T(8,128)(2,1)S(1)} %collective-permute-done.25), channel_id=1, source_target_pairs={{16,24},{17,25},{18,26},{19,27},{20,28},{21,29},{22,30},{23,31}} | collective-permute-start | bytes 1572872 | tf_op jit(solution)/shard_map/ppermute | solution.py:36
  226.9 13.1 %collective-permute-start.29 = (bf16[256,1024]{1,0:T(8,128)(2,1)S(1)}, bf16[256,1024]{1,0:T(8,128)(2,1)}, u32[]{:S(2)}, u32[]{:S(2)}) collective-permute-start(bf16[256,1024]{1,0:T(8,128)(2,1)S(1)} %collective-permute-done.26), channel_id=1, source_target_pairs={{8,0},{9,1},{10,2},{11,3},{12,4},{13,5},{14,6},{15,7}} | collective-permute-start | bytes 1572872 | tf_op jit(solution)/shard_map/ppermute | solution.py:36
  228.2 17.9 %collective-permute-start.21 = (bf16[256,1024]{1,0:T(8,128)(2,1)S(1)}, bf16[256,1024]{1,0:T(8,128)(2,1)S(1)}, u32[]{:S(2)}, u32[]{:S(2)}) collective-permute-start(bf16[256,1024]{1,0:T(8,128)(2,1)S(1)} %get-tuple-element.9), channel_id=1, source_target_pairs={{0,4},{1,5},{2,6},{3,7},{4,0},{5,1},{6,2},{7,3},{8,12},{9,13},{10,... | collective-permute-start | bytes 1572872 | tf_op jit(solution)/shard_map/ppermute | solution.py:36
  241.2 14.9 %collective-permute-start.24 = (bf16[256,1024]{1,0:T(8,128)(2,1)S(1)}, bf16[256,1024]{1,0:T(8,128)(2,1)S(1)}, u32[]{:S(2)}, u32[]{:S(2)}) collective-permute-start(bf16[256,1024]{1,0:T(8,128)(2,1)S(1)} %get-tuple-element.10), channel_id=1, source_target_pairs={{0,4},{1,5},{2,6},{3,7},{4,0},{5,1},{6,2},{7,3},{8,12},{9,13},{10,... | collective-permute-start | bytes 1572872 | tf_op jit(solution)/shard_map/ppermute | solution.py:36
  242.5 24.9 %collective-permute-start.27 = (bf16[256,1024]{1,0:T(8,128)(2,1)S(1)}, bf16[256,1024]{1,0:T(8,128)(2,1)S(1)}, u32[]{:S(2)}, u32[]{:S(2)}) collective-permute-start(bf16[256,1024]{1,0:T(8,128)(2,1)S(1)} %get-tuple-element.11), channel_id=1, source_target_pairs={{0,4},{1,5},{2,6},{3,7},{4,0},{5,1},{6,2},{7,3},{8,12},{9,13},{10,... | collective-permute-start | bytes 1572872 | tf_op jit(solution)/shard_map/ppermute | solution.py:36
  243.3 30.7 %collective-permute-start.30 = (bf16[256,1024]{1,0:T(8,128)(2,1)S(1)}, bf16[256,1024]{1,0:T(8,128)(2,1)S(1)}, u32[]{:S(2)}, u32[]{:S(2)}) collective-permute-start(bf16[256,1024]{1,0:T(8,128)(2,1)S(1)} %get-tuple-element.12), channel_id=1, source_target_pairs={{0,4},{1,5},{2,6},{3,7},{4,0},{5,1},{6,2},{7,3},{8,12},{9,13},{10,... | collective-permute-start | bytes 1572872 | tf_op jit(solution)/shard_map/ppermute | solution.py:36
  246.1 117.5 %collective-permute-start.32 = (bf16[4,256,1024]{2,1,0:T(8,128)(2,1)}, bf16[4,256,1024]{2,1,0:T(8,128)(2,1)}, u32[]{:S(2)}, u32[]{:S(2)}) collective-permute-start(bf16[4,256,1024]{2,1,0:T(8,128)(2,1)} %pad_maximum_fusion.1.refs_3_), channel_id=1, source_target_pairs={{0,1},{1,0},{2,3},{3,2},{4,5},{5,4},{6,7},{7,6},{8,9},{9,8},{10,11... | collective-permute-start | bytes 6291464 | tf_op jit(solution)/shard_map/ppermute | solution.py:39
  246.1 30.9 %collective-permute-start.34 = (bf16[256,1024]{1,0:T(8,128)(2,1)S(1)}, bf16[256,1024]{1,0:T(8,128)(2,1)S(1)}, u32[]{:S(2)}, u32[]{:S(2)}) collective-permute-start(bf16[256,1024]{1,0:T(8,128)(2,1)S(1)} %get-tuple-element.9), channel_id=1, source_target_pairs={{0,2},{1,3},{2,0},{3,1},{4,6},{5,7},{6,4},{7,5},{8,10},{9,11},{10,... | collective-permute-start | bytes 1572872 | tf_op jit(solution)/shard_map/ppermute | solution.py:39
  256.1 21.4 %collective-permute-start.35 = (bf16[256,1024]{1,0:T(8,128)(2,1)S(1)}, bf16[256,1024]{1,0:T(8,128)(2,1)S(1)}, u32[]{:S(2)}, u32[]{:S(2)}) collective-permute-start(bf16[256,1024]{1,0:T(8,128)(2,1)S(1)} %get-tuple-element.10), channel_id=1, source_target_pairs={{0,2},{1,3},{2,0},{3,1},{4,6},{5,7},{6,4},{7,5},{8,10},{9,11},{10,... | collective-permute-start | bytes 1572872 | tf_op jit(solution)/shard_map/ppermute | solution.py:39
  267.3 16.1 %collective-permute-start.36 = (bf16[256,1024]{1,0:T(8,128)(2,1)S(1)}, bf16[256,1024]{1,0:T(8,128)(2,1)S(1)}, u32[]{:S(2)}, u32[]{:S(2)}) collective-permute-start(bf16[256,1024]{1,0:T(8,128)(2,1)S(1)} %get-tuple-element.11), channel_id=1, source_target_pairs={{0,2},{1,3},{2,0},{3,1},{4,6},{5,7},{6,4},{7,5},{8,10},{9,11},{10,... | collective-permute-start | bytes 1572872 | tf_op jit(solution)/shard_map/ppermute | solution.py:39
  274.0 20.6 %collective-permute-start.37 = (bf16[256,1024]{1,0:T(8,128)(2,1)S(1)}, bf16[256,1024]{1,0:T(8,128)(2,1)S(1)}, u32[]{:S(2)}, u32[]{:S(2)}) collective-permute-start(bf16[256,1024]{1,0:T(8,128)(2,1)S(1)} %get-tuple-element.12), channel_id=1, source_target_pairs={{0,2},{1,3},{2,0},{3,1},{4,6},{5,7},{6,4},{7,5},{8,10},{9,11},{10,... | collective-permute-start | bytes 1572872 | tf_op jit(solution)/shard_map/ppermute | solution.py:39
  275.9 83.2 %copy-start.8 = (s32[1024]{0:T(1024)S(1)}, s32[1024]{0:T(1024)}, u32[]{:S(2)}) copy-start(s32[1024]{0:T(1024)} %param.29) | copy-start | bytes 12292
  277.0 83.5 %collective-permute-start.33 = (bf16[4,128,1024]{2,1,0:T(8,128)(2,1)}, bf16[4,128,1024]{2,1,0:T(8,128)(2,1)}, u32[]{:S(2)}, u32[]{:S(2)}) collective-permute-start(bf16[4,128,1024]{2,1,0:T(8,128)(2,1)} %slice.90), channel_id=1, source_target_pairs={{0,2},{1,3},{2,0},{3,1},{4,6},{5,7},{6,4},{7,5},{8,10},{9,11},{10,... | collective-permute-start | bytes 3145736 | tf_op jit(solution)/shard_map/ppermute | solution.py:39
  296.2 85.5 %collective-permute-start.40 = (bf16[4,256,1024]{2,1,0:T(8,128)(2,1)}, bf16[4,256,1024]{2,1,0:T(8,128)(2,1)}, u32[]{:S(2)}, u32[]{:S(2)}) collective-permute-start(bf16[4,256,1024]{2,1,0:T(8,128)(2,1)} %pad_maximum_fusion.2.refs_3_), channel_id=1, source_target_pairs={{0,1},{1,0},{2,3},{3,2},{4,5},{5,4},{6,7},{7,6},{8,9},{9,8},{10,11... | collective-permute-start | bytes 6291464 | tf_op jit(solution)/shard_map/ppermute | solution.py:39
  298.5 63.2 %collective-permute-start.38 = (bf16[4,128,1024]{2,1,0:T(8,128)(2,1)}, bf16[4,128,1024]{2,1,0:T(8,128)(2,1)}, u32[]{:S(2)}, u32[]{:S(2)}) collective-permute-start(bf16[4,128,1024]{2,1,0:T(8,128)(2,1)} %slice.91), channel_id=1, source_target_pairs={{0,4},{1,5},{2,6},{3,7},{4,0},{5,1},{6,2},{7,3},{8,12},{9,13},{10,... | collective-permute-start | bytes 3145736 | tf_op jit(solution)/shard_map/ppermute | solution.py:36
  299.4 1.3 collective-permute-start.16
  300.8 16.0 %collective-permute-start.17 = (f32[4,256]{1,0:T(4,128)S(1)}, f32[4,256]{1,0:T(4,128)S(1)}, u32[]{:S(2)}, u32[]{:S(2)}) collective-permute-start(f32[4,256]{1,0:T(4,128)S(1)} %add.269), channel_id=1, source_target_pairs={{0,2},{1,3},{2,0},{3,1},{4,6},{5,7},{6,4},{7,5},{8,10},{9,11},{10,... | collective-permute-start | bytes 12296 | tf_op jit(solution)/shard_map/ppermute | solution.py:39
  316.8 7.7 %collective-permute-start.18 = (f32[4,256]{1,0:T(4,128)S(1)}, f32[4,256]{1,0:T(4,128)S(1)}, u32[]{:S(2)}, u32[]{:S(2)}) collective-permute-start(f32[4,256]{1,0:T(4,128)S(1)} %add.270), channel_id=1, source_target_pairs={{0,4},{1,5},{2,6},{3,7},{4,0},{5,1},{6,2},{7,3},{8,12},{9,13},{10,... | collective-permute-start | bytes 12296 | tf_op jit(solution)/shard_map/ppermute | solution.py:36
  324.5 3.6 collective-permute-start.19
  328.1 32.1 %collective-permute-start.20 = (f32[4,256]{1,0:T(4,128)S(1)}, f32[4,256]{1,0:T(4,128)S(1)}, u32[]{:S(2)}, u32[]{:S(2)}) collective-permute-start(f32[4,256]{1,0:T(4,128)S(1)} %add.272), channel_id=1, source_target_pairs={{0,16},{1,17},{2,18},{3,19},{4,20},{5,21},{6,22},{7,23},{8,24},{9,... | collective-permute-start | bytes 12296 | tf_op jit(solution)/shard_map/ppermute | solution.py:36
  360.2 39.5 %collective-permute-start.31 = (bf16[4,256,1024]{2,1,0:T(8,128)(2,1)S(1)}, bf16[4,256,1024]{2,1,0:T(8,128)(2,1)}, u32[]{:S(2)}, u32[]{:S(2)}) collective-permute-start(bf16[4,256,1024]{2,1,0:T(8,128)(2,1)S(1)} %pad_maximum_fusion.own_ref), channel_id=1, source_target_pairs={{0,1},{1,0},{2,3},{3,2},{4,5},{5,4},{6,7},{7,6},{8,9},{9,8},{10,11... | collective-permute-start | bytes 6291464 | tf_op jit(solution)/shard_map/ppermute | solution.py:39
  363.1 55.9 %collective-permute-start.39 = (bf16[4,256,1024]{2,1,0:T(8,128)(2,1)S(1)}, bf16[4,256,1024]{2,1,0:T(8,128)(2,1)S(1)}, u32[]{:S(2)}, u32[]{:S(2)}) collective-permute-start(bf16[4,256,1024]{2,1,0:T(8,128)(2,1)S(1)} %constant_dynamic-update-slice_fusion.own_ref), channel_id=1, source_target_pairs={{0,1},{1,0},{2,3},{3,2},{4,5},{5,4},{6,7},{7,6},{8,9},{9,8},{10,11... | collective-permute-start | bytes 6291464 | tf_op jit(solution)/shard_map/ppermute | solution.py:39
  438.4 1.2 collective-permute-start.41
  439.6 3.8 collective-permute-start.42
  443.5 3.8 collective-permute-start.43
  447.4 3.8 collective-permute-start.44
  451.2 4.7 %collective-permute-start.45 = (f32[3,1024]{1,0:T(4,128)S(1)}, f32[3,1024]{1,0:T(4,128)S(1)}, u32[]{:S(2)}, u32[]{:S(2)}) collective-permute-start(f32[3,1024]{1,0:T(4,128)S(1)} %pad_maximum_fusion.9), channel_id=1, source_target_pairs={{0,16},{1,17},{2,18},{3,19},{4,20},{5,21},{6,22},{7,23},{8,24},{9,... | collective-permute-start | bytes 36872 | tf_op jit(solution)/shard_map/ppermute | solution.py:36
  (16 other events, 720.5 us)
